TPU v7x, 32 devices: a whole 2x2x4 slice. The times are simulated.
32 devices in a mesh: head: 2 (over x), seq: 16 (over z, y, core).
Axes of the slice: x: 2, y: 2, z: 4, core: 2. Of those that a mesh axis runs over, the one named last changes fastest.
Arguments:
- query_rows: bfloat16 [16, 2, 256, 256], P('seq', 'head'), may hold values from -6 to 6
- key_rows: bfloat16 [16, 2, 256, 256], P('seq', 'head'), may hold values from -6 to 6
- value_rows: bfloat16 [16, 2, 256, 256], P('seq', 'head'), may hold values from -6 to 6
- output_grad: bfloat16 [16, 2, 256, 256], P('seq', 'head'), may hold values from -384 to 384
- output_rows: bfloat16 [16, 2, 256, 256], P('seq', 'head'), may hold values from -1.5 to 1.5
- row_logsumexp: float32 [8192, 2], P('seq', 'head')
- chosen_owner: int32 [128, 2], P('seq'), may hold values from 0 to 15, all different within a row; in each aligned block of 8 rows (0 to 7, 8 to 15, ...) at most 2 rows name the same one
- chosen_cubes: int32 [128, 2, 8], P('seq'), may hold values 0 or 1
Outputs:
- query_grad: bfloat16 [16, 2, 256, 256], P('seq', 'head')
- key_grad: bfloat16 [16, 2, 256, 256], P('seq', 'head')
- value_grad: bfloat16 [16, 2, 256, 256], P('seq', 'head')
Inputs may be any that keep to these rules, and one draw needn't show every extreme that they name: `chosen_owner`: each query cube names 2 different indices; the 8 query cubes held by one index of seq name any one index at most 2 times, and exactly 2 times for some index in every draw. `chosen_cubes`: 1 marks a selected key cube.
All inputs are finite; a program needn't handle non-finite values. No bound on the sum of `chosen_cubes` on one device may be relied on, other than what follows from the above.
Results may differ from a plain program's by a relative error of at most 0.0053.
Values may be sent and summed in bfloat16 or wider, within the bound.
A program may use at most 64 MiB of HBM per device.

v0:
```python
import math

import jax
import jax.numpy as jnp
from jax import lax
from jax.sharding import PartitionSpec as P

CAP = 2


def slot_pass(key_local, value_local, query_in, grad_in, log_in, delta_in, keep_in, cube_rows):
    slot_count = query_in.shape[0]
    head_width = query_in.shape[2]
    block_rows = math.gcd(slot_count, max(1, 512 // cube_rows))
    blocks = slot_count // block_rows
    softmax_scale = 1.0 / math.sqrt(head_width)

    def slot_step(totals, pieces):
        grad_k, grad_v = totals
        query_part, grad_part, log_part, delta_part, keep_part = pieces
        scores = (
            jnp.einsum("brd,kd->brk", query_part, key_local, preferred_element_type=jnp.float32)
            * softmax_scale
        )
        key_keep = jnp.repeat(keep_part, cube_rows, axis=1)
        weights = jnp.exp(scores - log_part[:, :, None]) * key_keep[:, None, :]
        dweights = jnp.einsum(
            "brd,kd->brk", grad_part, value_local, preferred_element_type=jnp.float32
        )
        dscores = weights * (dweights - delta_part[:, :, None])
        weights_low = weights.astype(jnp.bfloat16)
        dscores_low = dscores.astype(jnp.bfloat16)
        grad_v = grad_v + jnp.einsum(
            "brk,brd->kd", weights_low, grad_part, preferred_element_type=jnp.float32
        )
        grad_k = grad_k + softmax_scale * jnp.einsum(
            "brk,brd->kd", dscores_low, query_part, preferred_element_type=jnp.float32
        )
        grad_q = softmax_scale * jnp.einsum(
            "brk,kd->brd", dscores_low, key_local, preferred_element_type=jnp.float32
        )
        return ((grad_k, grad_v), grad_q)

    def blocked(array):
        return array.reshape((blocks, block_rows) + array.shape[1:])

    zero_init = jnp.zeros(key_local.shape, jnp.float32)
    inputs = (
        blocked(query_in),
        blocked(grad_in),
        blocked(log_in),
        blocked(delta_in),
        blocked(keep_in),
    )
    (grad_k, grad_v), grad_q = lax.scan(slot_step, (zero_init, zero_init), inputs)
    return (grad_k, grad_v, grad_q.reshape(query_in.shape))


def on_device(
    query_rows,
    key_rows,
    value_rows,
    output_grad,
    output_rows,
    row_logsumexp,
    chosen_owner,
    chosen_cubes,
):
    head_count = lax.axis_size("head")
    seq_count = lax.axis_size("seq")
    piece_rows = query_rows.shape[2]
    head_width = query_rows.shape[3] // head_count

    def split_heads(array):
        return array.reshape(piece_rows, head_count, head_width)

    gathered = (
        lax.all_to_all(split_heads(query_rows), "head", split_axis=1, concat_axis=0, tiled=True),
        lax.all_to_all(split_heads(key_rows), "head", split_axis=1, concat_axis=0, tiled=True),
        lax.all_to_all(split_heads(value_rows), "head", split_axis=1, concat_axis=0, tiled=True),
        lax.all_to_all(split_heads(output_grad), "head", split_axis=1, concat_axis=0, tiled=True),
        lax.all_to_all(split_heads(output_rows), "head", split_axis=1, concat_axis=0, tiled=True),
    )
    query_tok, key_tok, value_tok, grad_tok, output_tok = [
        member.reshape(-1, head_width) for member in gathered
    ]
    cube_local = chosen_owner.shape[0]
    token_local = query_tok.shape[0]
    cube_rows = token_local // cube_local
    log_total = row_logsumexp[:, 0]
    row_delta = jnp.sum(grad_tok.astype(jnp.float32) * output_tok.astype(jnp.float32), axis=1)
    targets = jnp.arange(seq_count, dtype=jnp.int32)
    matches = (chosen_owner[:, :, None] == targets[None, None, :]).astype(jnp.int32)
    touched = jnp.sum(matches, axis=1)
    position = jnp.cumsum(touched, axis=0) - 1
    slot_ids = jnp.arange(CAP, dtype=jnp.int32)
    placing = (
        (touched[:, :, None] == 1) & (position[:, :, None] == slot_ids[None, None, :])
    ).astype(jnp.float32)
    slot_table = jnp.transpose(placing, (1, 2, 0))
    cube_choice = jnp.einsum(
        "xjn,xjk->xnk",
        matches.astype(jnp.float32),
        chosen_cubes.astype(jnp.float32),
        precision=lax.Precision.HIGHEST,
    )
    keep_send = jnp.einsum("ncx,xnk->nck", slot_table, cube_choice, precision=lax.Precision.HIGHEST)
    table_low = slot_table.astype(jnp.bfloat16)
    query_cubes = query_tok.reshape(cube_local, cube_rows, head_width)
    grad_cubes = grad_tok.reshape(cube_local, cube_rows, head_width)
    query_send = jnp.einsum(
        "ncx,xrd->ncrd", table_low, query_cubes, preferred_element_type=jnp.float32
    ).astype(jnp.bfloat16)
    grad_send = jnp.einsum(
        "ncx,xrd->ncrd", table_low, grad_cubes, preferred_element_type=jnp.float32
    ).astype(jnp.bfloat16)
    log_send = jnp.einsum(
        "ncx,xr->ncr",
        slot_table,
        log_total.reshape(cube_local, cube_rows),
        precision=lax.Precision.HIGHEST,
    )
    delta_send = jnp.einsum(
        "ncx,xr->ncr",
        slot_table,
        row_delta.reshape(cube_local, cube_rows),
        precision=lax.Precision.HIGHEST,
    )
    moved_query, moved_grad = (
        lax.all_to_all(query_send, "seq", split_axis=0, concat_axis=0, tiled=True),
        lax.all_to_all(grad_send, "seq", split_axis=0, concat_axis=0, tiled=True),
    )
    moved_log, moved_delta, moved_keep = (
        lax.all_to_all(log_send, "seq", split_axis=0, concat_axis=0, tiled=True),
        lax.all_to_all(delta_send, "seq", split_axis=0, concat_axis=0, tiled=True),
        lax.all_to_all(keep_send, "seq", split_axis=0, concat_axis=0, tiled=True),
    )
    grad_k, grad_v, grad_q = slot_pass(
        key_tok,
        value_tok,
        moved_query.reshape(-1, cube_rows, head_width),
        moved_grad.reshape(-1, cube_rows, head_width),
        moved_log.reshape(-1, cube_rows),
        moved_delta.reshape(-1, cube_rows),
        moved_keep.reshape(-1, cube_local),
        cube_rows,
    )
    returned = lax.all_to_all(
        grad_q.reshape(seq_count, CAP, cube_rows, head_width),
        "seq",
        split_axis=0,
        concat_axis=0,
        tiled=True,
    )
    query_grad = jnp.einsum(
        "ncx,ncrd->xrd", slot_table, returned, precision=lax.Precision.HIGHEST
    ).reshape(token_local, head_width)
    outputs = (
        query_grad.astype(jnp.bfloat16)[:, None, :],
        grad_k.astype(jnp.bfloat16)[:, None, :],
        grad_v.astype(jnp.bfloat16)[:, None, :],
    )
    regrouped = (
        lax.all_to_all(outputs[0], "head", split_axis=0, concat_axis=1, tiled=True),
        lax.all_to_all(outputs[1], "head", split_axis=0, concat_axis=1, tiled=True),
        lax.all_to_all(outputs[2], "head", split_axis=0, concat_axis=1, tiled=True),
    )
    return tuple(
        (member.reshape(1, 1, piece_rows, head_count * head_width) for member in regrouped)
    )


def solution(mesh):
    placed = (
        P("seq", "head", None, None),
        P("seq", "head", None, None),
        P("seq", "head", None, None),
        P("seq", "head", None, None),
        P("seq", "head", None, None),
        P("seq", "head"),
        P("seq", None),
        P("seq", None, None),
    )
    return jax.shard_map(
        on_device,
        mesh=mesh,
        in_specs=placed,
        out_specs=(
            P("seq", "head", None, None),
            P("seq", "head", None, None),
            P("seq", "head", None, None),
        ),
        check_vma=False,
    )
```

profile of v0, /device:TPU:0, one launch (start us, length us, event | category | flops | bytes accessed | tf_op | source)
XLA Modules:
  0.0 174.7 jit_solution(15396943051404043775)
XLA Ops:
  0.6 0.8 copy.101
  1.6 0.6 copy-done.6
  2.6 0.8 fusion.45
  3.4 7.4 %all-to-all-start.4 = ((f32[16,2,8]{2,1,0:T(2,128)}), f32[16,2,8]{2,1,0:T(2,128)S(1)}, u32[]{:S(2)}, u32[]{:S(2)}) async-start(f32[16,2,8]{2,1,0:T(2,128)} %fusion.45), calls=%async_computation.4 | async-start | bytes 32768 | tf_op jit(solution)/shard_map/all_to_all | solution.py:136
  10.8 0.5 broadcast.57
  11.3 0.7 reduce.4
  12.3 0.7 reshape.118
  13.0 4.3 %all-to-all-done.4 = f32[16,2,8]{2,1,0:T(2,128)S(1)} async-done(((f32[16,2,8]{2,1,0:T(2,128)}), f32[16,2,8]{2,1,0:T(2,128)S(1)}, u32[]{:S(2)}, u32[]{:S(2)}) %all-to-all-start.4) | async-done | bytes 1056 | tf_op jit(solution)/shard_map/all_to_all | solution.py:136
  17.3 3.5 %all-to-all-start.3 = ((f32[16,1,128]{2,1,0:T(1,128)}), f32[16,1,128]{2,1,0:T(1,128)S(1)}, u32[]{:S(2)}, u32[]{:S(2)}) async-start(f32[16,1,128]{2,1,0:T(1,128)} %reshape.118), calls=%async_computation.3 | async-start | bytes 16384 | tf_op jit(solution)/shard_map/all_to_all | solution.py:134
  20.8 0.8 copy.102
  21.6 5.6 %all-to-all-done.3 = f32[16,1,128]{2,1,0:T(1,128)S(1)} async-done(((f32[16,1,128]{2,1,0:T(1,128)}), f32[16,1,128]{2,1,0:T(1,128)S(1)}, u32[]{:S(2)}, u32[]{:S(2)}) %all-to-all-start.3) | async-done | bytes 8224 | tf_op jit(solution)/shard_map/all_to_all | solution.py:134
  27.1 3.5 %all-to-all-start = ((bf16[256,2,128]{0,2,1:T(8,128)(2,1)}), bf16[256,2,128]{0,2,1:T(8,128)(2,1)S(1)}, u32[]{:S(2)}, u32[]{:S(2)}) async-start(bf16[256,2,128]{0,2,1:T(8,128)(2,1)} %bitcast.5), calls=%async_computation | async-start | bytes 262144 | tf_op jit(solution)/shard_map/all_to_all | solution.py:78
  30.7 0.8 copy.110
  31.4 3.7 %all-to-all-done = bf16[256,2,128]{0,2,1:T(8,128)(2,1)S(1)} async-done(((bf16[256,2,128]{0,2,1:T(8,128)(2,1)}), bf16[256,2,128]{0,2,1:T(8,128)(2,1)S(1)}, u32[]{:S(2)}, u32[]{:S(2)}) %all-to-all-start) | async-done | bytes 131104 | tf_op jit(solution)/shard_map/all_to_all | solution.py:78
  35.1 3.5 %all-to-all-start.5 = ((bf16[256,2,128]{0,2,1:T(8,128)(2,1)}), bf16[256,2,128]{0,2,1:T(8,128)(2,1)S(1)}, u32[]{:S(2)}, u32[]{:S(2)}) async-start(bf16[256,2,128]{0,2,1:T(8,128)(2,1)} %bitcast.17), calls=%async_computation.5 | async-start | bytes 262144 | tf_op jit(solution)/shard_map/all_to_all | solution.py:81
  38.6 0.8 copy.115
  39.4 3.7 %all-to-all-done.5 = bf16[256,2,128]{0,2,1:T(8,128)(2,1)S(1)} async-done(((bf16[256,2,128]{0,2,1:T(8,128)(2,1)}), bf16[256,2,128]{0,2,1:T(8,128)(2,1)S(1)}, u32[]{:S(2)}, u32[]{:S(2)}) %all-to-all-start.5) | async-done | bytes 131104 | tf_op jit(solution)/shard_map/all_to_all | solution.py:81
  43.1 3.5 %all-to-all-start.8 = ((bf16[256,2,128]{0,2,1:T(8,128)(2,1)}), bf16[256,2,128]{0,2,1:T(8,128)(2,1)S(1)}, u32[]{:S(2)}, u32[]{:S(2)}) async-start(bf16[256,2,128]{0,2,1:T(8,128)(2,1)} %bitcast.27), calls=%async_computation.8 | async-start | bytes 262144 | tf_op jit(solution)/shard_map/all_to_all | solution.py:82
  46.7 0.7 copy.106
  47.7 0.7 copy.114
  48.3 2.7 %all-to-all-done.8 = bf16[256,2,128]{0,2,1:T(8,128)(2,1)S(1)} async-done(((bf16[256,2,128]{0,2,1:T(8,128)(2,1)}), bf16[256,2,128]{0,2,1:T(8,128)(2,1)S(1)}, u32[]{:S(2)}, u32[]{:S(2)}) %all-to-all-start.8) | async-done | bytes 131104 | tf_op jit(solution)/shard_map/all_to_all | solution.py:82
  51.1 3.4 %all-to-all-start.2 = ((bf16[256,2,128]{2,0,1:T(8,128)(2,1)}), bf16[256,2,128]{2,0,1:T(8,128)(2,1)S(1)}, u32[]{:S(2)}, u32[]{:S(2)}) async-start(bf16[256,2,128]{2,0,1:T(8,128)(2,1)} %copy.106), calls=%async_computation.2 | async-start | bytes 262144 | tf_op jit(solution)/shard_map/all_to_all | solution.py:79
  54.6 4.3 %all-to-all-done.2 = bf16[256,2,128]{2,0,1:T(8,128)(2,1)S(1)} async-done(((bf16[256,2,128]{2,0,1:T(8,128)(2,1)}), bf16[256,2,128]{2,0,1:T(8,128)(2,1)S(1)}, u32[]{:S(2)}, u32[]{:S(2)}) %all-to-all-start.2) | async-done | bytes 131104 | tf_op jit(solution)/shard_map/all_to_all | solution.py:79
  58.9 3.4 %all-to-all-start.7 = ((bf16[256,2,128]{2,0,1:T(8,128)(2,1)}), bf16[256,2,128]{2,0,1:T(8,128)(2,1)S(1)}, u32[]{:S(2)}, u32[]{:S(2)}) async-start(bf16[256,2,128]{2,0,1:T(8,128)(2,1)} %copy.114), calls=%async_computation.7 | async-start | bytes 262144 | tf_op jit(solution)/shard_map/all_to_all | solution.py:80
  62.7 0.7 reshape.120
  63.3 3.4 %all-to-all-done.7 = bf16[256,2,128]{2,0,1:T(8,128)(2,1)S(1)} async-done(((bf16[256,2,128]{2,0,1:T(8,128)(2,1)}), bf16[256,2,128]{2,0,1:T(8,128)(2,1)S(1)}, u32[]{:S(2)}, u32[]{:S(2)}) %all-to-all-start.7) | async-done | bytes 131104 | tf_op jit(solution)/shard_map/all_to_all | solution.py:80
  66.8 3.5 %all-to-all-start.9 = ((f32[16,1,128]{2,1,0:T(1,128)}), f32[16,1,128]{2,1,0:T(1,128)S(1)}, u32[]{:S(2)}, u32[]{:S(2)}) async-start(f32[16,1,128]{2,1,0:T(1,128)} %reshape.120), calls=%async_computation.9 | async-start | bytes 16384 | tf_op jit(solution)/shard_map/all_to_all | solution.py:135
  70.6 0.9 copy.113
  71.5 5.0 %all-to-all-done.9 = f32[16,1,128]{2,1,0:T(1,128)S(1)} async-done(((f32[16,1,128]{2,1,0:T(1,128)}), f32[16,1,128]{2,1,0:T(1,128)S(1)}, u32[]{:S(2)}, u32[]{:S(2)}) %all-to-all-start.9) | async-done | bytes 8224 | tf_op jit(solution)/shard_map/all_to_all | solution.py:135
  76.6 3.6 %all-to-all-start.6 = ((bf16[16,2,64,128]{3,2,1,0:T(8,128)(2,1)}), bf16[16,2,64,128]{3,2,1,0:T(8,128)(2,1)S(1)}, u32[]{:S(2)}, u32[]{:S(2)}) async-start(bf16[16,2,64,128]{3,2,1,0:T(8,128)(2,1)} %copy.113), calls=%async_computation.6 | async-start | bytes 1048576 | tf_op jit(solution)/shard_map/all_to_all | solution.py:131
  80.6 0.9 copy.105
  81.6 12.8 %all-to-all-done.6 = bf16[16,2,64,128]{3,2,1,0:T(8,128)(2,1)S(1)} async-done(((bf16[16,2,64,128]{3,2,1,0:T(8,128)(2,1)}), bf16[16,2,64,128]{3,2,1,0:T(8,128)(2,1)S(1)}, u32[]{:S(2)}, u32[]{:S(2)}) %all-to-all-start.6) | async-done | bytes 524320 | tf_op jit(solution)/shard_map/all_to_all | solution.py:131
  94.4 4.1 %all-to-all-start.1 = ((bf16[16,2,64,128]{3,2,1,0:T(8,128)(2,1)}), bf16[16,2,64,128]{3,2,1,0:T(8,128)(2,1)S(1)}, u32[]{:S(2)}, u32[]{:S(2)}) async-start(bf16[16,2,64,128]{3,2,1,0:T(8,128)(2,1)} %copy.105), calls=%async_computation.1 | async-start | bytes 1048576 | tf_op jit(solution)/shard_map/all_to_all | solution.py:130
  98.5 0.5 broadcast.58
  99.0 0.7 reduce.5
  99.8 0.7 reduce.6
  100.5 12.2 %all-to-all-done.1 = bf16[16,2,64,128]{3,2,1,0:T(8,128)(2,1)S(1)} async-done(((bf16[16,2,64,128]{3,2,1,0:T(8,128)(2,1)}), bf16[16,2,64,128]{3,2,1,0:T(8,128)(2,1)S(1)}, u32[]{:S(2)}, u32[]{:S(2)}) %all-to-all-start.1) | async-done | bytes 524320 | tf_op jit(solution)/shard_map/all_to_all | solution.py:130
  112.8 7.8 %while.15 = (s32[]{:T(128)}, f32[512,128]{1,0:T(8,128)S(1)}, f32[512,128]{1,0:T(8,128)S(1)}, f32[4,8,64,128]{3,2,1,0:T(8,128)S(1)}, bf16[4,8,64,128]{3,2,1,0:T(8...) while((s32[]{:T(128)}, f32[512,128]{1,0:T(8,128)S(1)}, ...), condition=%wide.region_4.5_spmd.clone, body=%wide.region_3.4_spmd.clone.sunk | while | flops 337772544 | bytes 7029676 | solution.py:55
  113.3 0.4 fusion.83
  114.0 0.4 fusion.82
  115.2 0.4 fusion.83
  115.9 0.4 fusion.82
  117.9 0.4 fusion.82
  119.9 0.4 fusion.82
  120.6 0.5 broadcast.60
  121.2 0.7 reduce.9
  121.8 0.7 reshape.126
  122.5 3.4 %all-to-all-start.13 = ((bf16[2,2,16384]{2,1,0:T(2,128)(2,1)}), bf16[2,2,16384]{2,1,0:T(2,128)(2,1)S(1)}, u32[]{:S(2)}, u32[]{:S(2)}) async-start(bf16[2,2,16384]{2,1,0:T(2,128)(2,1)} %reshape.126), calls=%async_computation.13 | async-start | bytes 262144 | tf_op jit(solution)/shard_map/all_to_all | solution.py:166
  125.9 1.8 %copy.117 = f32[16,2,64,128]{3,1,2,0:T(2,128)} copy(f32[16,2,64,128]{3,2,1,0:T(8,128)S(1)} %bitcast.162) | data formatting | bytes 2097152 | tf_op jit(solution)/shard_map/reshape;reshape | solution.py:149
  127.7 2.7 %all-to-all-done.13 = bf16[2,2,16384]{2,1,0:T(2,128)(2,1)S(1)} async-done(((bf16[2,2,16384]{2,1,0:T(2,128)(2,1)}), bf16[2,2,16384]{2,1,0:T(2,128)(2,1)S(1)}, u32[]{:S(2)}, u32[]{:S(2)}) %all-to-all-start.13) | async-done | bytes 131104 | tf_op jit(solution)/shard_map/all_to_all | solution.py:166
  130.4 4.3 %all-to-all-start.10 = ((f32[16,2,64,128]{3,1,2,0:T(2,128)}), f32[16,2,64,128]{3,1,2,0:T(2,128)S(1)}, u32[]{:S(2)}, u32[]{:S(2)}) async-start(f32[16,2,64,128]{3,1,2,0:T(2,128)} %copy.117), calls=%async_computation.10 | async-start | bytes 2097152 | tf_op jit(solution)/shard_map/all_to_all | solution.py:148
  134.7 0.7 reduce.8
  135.4 0.7 reshape.124
  136.0 21.5 %all-to-all-done.10 = f32[16,2,64,128]{3,1,2,0:T(2,128)S(1)} async-done(((f32[16,2,64,128]{3,1,2,0:T(2,128)}), f32[16,2,64,128]{3,1,2,0:T(2,128)S(1)}, u32[]{:S(2)}, u32[]{:S(2)}) %all-to-all-start.10) | async-done | bytes 1048608 | tf_op jit(solution)/shard_map/all_to_all | solution.py:148
  157.6 3.4 %all-to-all-start.12 = ((bf16[2,2,16384]{2,1,0:T(2,128)(2,1)}), bf16[2,2,16384]{2,1,0:T(2,128)(2,1)S(1)}, u32[]{:S(2)}, u32[]{:S(2)}) async-start(bf16[2,2,16384]{2,1,0:T(2,128)(2,1)} %reshape.124), calls=%async_computation.12 | async-start | bytes 262144 | tf_op jit(solution)/shard_map/all_to_all | solution.py:165
  160.9 1.0 fusion.26
  162.0 0.7 reduce.7
  162.7 0.7 reshape.122
  163.4 2.4 %all-to-all-done.12 = bf16[2,2,16384]{2,1,0:T(2,128)(2,1)S(1)} async-done(((bf16[2,2,16384]{2,1,0:T(2,128)(2,1)}), bf16[2,2,16384]{2,1,0:T(2,128)(2,1)S(1)}, u32[]{:S(2)}, u32[]{:S(2)}) %all-to-all-start.12) | async-done | bytes 131104 | tf_op jit(solution)/shard_map/all_to_all | solution.py:165
  165.8 3.4 %all-to-all-start.11 = ((bf16[2,2,16384]{2,1,0:T(2,128)(2,1)}), bf16[2,2,16384]{2,1,0:T(2,128)(2,1)S(1)}, u32[]{:S(2)}, u32[]{:S(2)}) async-start(bf16[2,2,16384]{2,1,0:T(2,128)(2,1)} %reshape.122), calls=%async_computation.11 | async-start | bytes 262144 | tf_op jit(solution)/shard_map/all_to_all | solution.py:164
  169.5 0.8 copy.127
  170.5 0.8 copy.128
  171.3 2.4 %all-to-all-done.11 = bf16[2,2,16384]{2,1,0:T(2,128)(2,1)S(1)} async-done(((bf16[2,2,16384]{2,1,0:T(2,128)(2,1)}), bf16[2,2,16384]{2,1,0:T(2,128)(2,1)S(1)}, u32[]{:S(2)}, u32[]{:S(2)}) %all-to-all-start.11) | async-done | bytes 131104 | tf_op jit(solution)/shard_map/all_to_all | solution.py:164
  174.0 0.8 copy.126
  (80 shorter events, 8.7 us)
Async XLA Ops:
  1.5 0.7 copy-start.6
  2.5 8.9 %copy-start.5 = (f32[512,1]{0,1:T(1,128)S(1)}, f32[512,1]{0,1:T(1,128)}, u32[]{:S(2)}) copy-start(f32[512,1]{0,1:T(1,128)} %param.15) | copy-start | bytes 6148
  2.6 18.2 %copy-start = (bf16[1,1,256,256]{3,2,1,0:T(8,128)(2,1)S(1)}, bf16[1,1,256,256]{3,2,1,0:T(8,128)(2,1)}, u32[]{:S(2)}) copy-start(bf16[1,1,256,256]{3,2,1,0:T(8,128)(2,1)} %param.10) | copy-start | bytes 393220
  3.4 13.9 %all-to-all-start.4 = ((f32[16,2,8]{2,1,0:T(2,128)}), f32[16,2,8]{2,1,0:T(2,128)S(1)}, u32[]{:S(2)}, u32[]{:S(2)}) async-start(f32[16,2,8]{2,1,0:T(2,128)} %fusion.45), calls=%async_computation.4 | async-start | bytes 32768 | tf_op jit(solution)/shard_map/all_to_all | solution.py:136
  17.3 9.8 %all-to-all-start.3 = ((f32[16,1,128]{2,1,0:T(1,128)}), f32[16,1,128]{2,1,0:T(1,128)S(1)}, u32[]{:S(2)}, u32[]{:S(2)}) async-start(f32[16,1,128]{2,1,0:T(1,128)} %reshape.118), calls=%async_computation.3 | async-start | bytes 16384 | tf_op jit(solution)/shard_map/all_to_all | solution.py:134
  27.1 3.5 %copy-start.1 = (bf16[1,1,256,256]{3,2,1,0:T(8,128)(2,1)S(1)}, bf16[1,1,256,256]{3,2,1,0:T(8,128)(2,1)}, u32[]{:S(2)}) copy-start(bf16[1,1,256,256]{3,2,1,0:T(8,128)(2,1)} %param.13) | copy-start | bytes 393220
  27.1 8.0 %all-to-all-start = ((bf16[256,2,128]{0,2,1:T(8,128)(2,1)}), bf16[256,2,128]{0,2,1:T(8,128)(2,1)S(1)}, u32[]{:S(2)}, u32[]{:S(2)}) async-start(bf16[256,2,128]{0,2,1:T(8,128)(2,1)} %bitcast.5), calls=%async_computation | async-start | bytes 262144 | tf_op jit(solution)/shard_map/all_to_all | solution.py:78
  35.1 3.5 %copy-start.2 = (bf16[1,1,256,256]{3,2,1,0:T(8,128)(2,1)S(1)}, bf16[1,1,256,256]{3,2,1,0:T(8,128)(2,1)}, u32[]{:S(2)}) copy-start(bf16[1,1,256,256]{3,2,1,0:T(8,128)(2,1)} %param.14) | copy-start | bytes 393220
  35.1 8.0 %all-to-all-start.5 = ((bf16[256,2,128]{0,2,1:T(8,128)(2,1)}), bf16[256,2,128]{0,2,1:T(8,128)(2,1)S(1)}, u32[]{:S(2)}, u32[]{:S(2)}) async-start(bf16[256,2,128]{0,2,1:T(8,128)(2,1)} %bitcast.17), calls=%async_computation.5 | async-start | bytes 262144 | tf_op jit(solution)/shard_map/all_to_all | solution.py:81
  43.1 3.5 %copy-start.3 = (bf16[1,1,256,256]{3,2,1,0:T(8,128)(2,1)S(1)}, bf16[1,1,256,256]{3,2,1,0:T(8,128)(2,1)}, u32[]{:S(2)}) copy-start(bf16[1,1,256,256]{3,2,1,0:T(8,128)(2,1)} %param.11) | copy-start | bytes 393220
  43.1 8.0 %all-to-all-start.8 = ((bf16[256,2,128]{0,2,1:T(8,128)(2,1)}), bf16[256,2,128]{0,2,1:T(8,128)(2,1)S(1)}, u32[]{:S(2)}, u32[]{:S(2)}) async-start(bf16[256,2,128]{0,2,1:T(8,128)(2,1)} %bitcast.27), calls=%async_computation.8 | async-start | bytes 262144 | tf_op jit(solution)/shard_map/all_to_all | solution.py:82
  46.7 1.0 copy-start.4
  51.1 7.8 %all-to-all-start.2 = ((bf16[256,2,128]{2,0,1:T(8,128)(2,1)}), bf16[256,2,128]{2,0,1:T(8,128)(2,1)S(1)}, u32[]{:S(2)}, u32[]{:S(2)}) async-start(bf16[256,2,128]{2,0,1:T(8,128)(2,1)} %copy.106), calls=%async_computation.2 | async-start | bytes 262144 | tf_op jit(solution)/shard_map/all_to_all | solution.py:79
  58.9 7.8 %all-to-all-start.7 = ((bf16[256,2,128]{2,0,1:T(8,128)(2,1)}), bf16[256,2,128]{2,0,1:T(8,128)(2,1)S(1)}, u32[]{:S(2)}, u32[]{:S(2)}) async-start(bf16[256,2,128]{2,0,1:T(8,128)(2,1)} %copy.114), calls=%async_computation.7 | async-start | bytes 262144 | tf_op jit(solution)/shard_map/all_to_all | solution.py:80
  66.8 9.8 %all-to-all-start.9 = ((f32[16,1,128]{2,1,0:T(1,128)}), f32[16,1,128]{2,1,0:T(1,128)S(1)}, u32[]{:S(2)}, u32[]{:S(2)}) async-start(f32[16,1,128]{2,1,0:T(1,128)} %reshape.120), calls=%async_computation.9 | async-start | bytes 16384 | tf_op jit(solution)/shard_map/all_to_all | solution.py:135
  76.6 17.8 %all-to-all-start.6 = ((bf16[16,2,64,128]{3,2,1,0:T(8,128)(2,1)}), bf16[16,2,64,128]{3,2,1,0:T(8,128)(2,1)S(1)}, u32[]{:S(2)}, u32[]{:S(2)}) async-start(bf16[16,2,64,128]{3,2,1,0:T(8,128)(2,1)} %copy.113), calls=%async_computation.6 | async-start | bytes 1048576 | tf_op jit(solution)/shard_map/all_to_all | solution.py:131
  94.4 18.4 %all-to-all-start.1 = ((bf16[16,2,64,128]{3,2,1,0:T(8,128)(2,1)}), bf16[16,2,64,128]{3,2,1,0:T(8,128)(2,1)S(1)}, u32[]{:S(2)}, u32[]{:S(2)}) async-start(bf16[16,2,64,128]{3,2,1,0:T(8,128)(2,1)} %copy.105), calls=%async_computation.1 | async-start | bytes 1048576 | tf_op jit(solution)/shard_map/all_to_all | solution.py:130
  122.5 7.8 %all-to-all-start.13 = ((bf16[2,2,16384]{2,1,0:T(2,128)(2,1)}), bf16[2,2,16384]{2,1,0:T(2,128)(2,1)S(1)}, u32[]{:S(2)}, u32[]{:S(2)}) async-start(bf16[2,2,16384]{2,1,0:T(2,128)(2,1)} %reshape.126), calls=%async_computation.13 | async-start | bytes 262144 | tf_op jit(solution)/shard_map/all_to_all | solution.py:166
  130.4 27.2 %all-to-all-start.10 = ((f32[16,2,64,128]{3,1,2,0:T(2,128)}), f32[16,2,64,128]{3,1,2,0:T(2,128)S(1)}, u32[]{:S(2)}, u32[]{:S(2)}) async-start(f32[16,2,64,128]{3,1,2,0:T(2,128)} %copy.117), calls=%async_computation.10 | async-start | bytes 2097152 | tf_op jit(solution)/shard_map/all_to_all | solution.py:148
  157.6 8.3 %all-to-all-start.12 = ((bf16[2,2,16384]{2,1,0:T(2,128)(2,1)}), bf16[2,2,16384]{2,1,0:T(2,128)(2,1)S(1)}, u32[]{:S(2)}, u32[]{:S(2)}) async-start(bf16[2,2,16384]{2,1,0:T(2,128)(2,1)} %reshape.124), calls=%async_computation.12 | async-start | bytes 262144 | tf_op jit(solution)/shard_map/all_to_all | solution.py:165
  165.8 7.8 %all-to-all-start.11 = ((bf16[2,2,16384]{2,1,0:T(2,128)(2,1)}), bf16[2,2,16384]{2,1,0:T(2,128)(2,1)S(1)}, u32[]{:S(2)}, u32[]{:S(2)}) async-start(bf16[2,2,16384]{2,1,0:T(2,128)(2,1)} %reshape.122), calls=%async_computation.11 | async-start | bytes 262144 | tf_op jit(solution)/shard_map/all_to_all | solution.py:164
where the time goes:
time: 177 us; the launch traced here: 175 us
  waiting for transfers between devices  86.9 us (49%)
  starting transfers between devices  53.7 us (30%)
  local copies, waits for them, and re-layouts  18.4 us (10%)
  matrix products  10.1 us (6%)
  other arithmetic  4.25 us (2%)
    all_to_all x1, waiting for transfers between devices, on_device(): lax.all_to_all(grad_q.reshape(seq_count, CAP, cube_rows, head_width), 'se...  21.5 us
    all_to_all x1, waiting for transfers between devices, on_device(): lax.all_to_all(grad_send, 'seq', split_axis=0, concat_axis=0, tiled=True)  12.8 us
    all_to_all x1, waiting for transfers between devices, on_device(): lax.all_to_all(query_send, 'seq', split_axis=0, concat_axis=0, tiled=True)  12.2 us
    unnamed x35, local copies, waits for them, and re-layouts  10.7 us
    all_to_all x1, starting transfers between devices, on_device(): lax.all_to_all(keep_send, 'seq', split_axis=0, concat_axis=0, tiled=True)  7.41 us
    all_to_all x1, waiting for transfers between devices, on_device(): lax.all_to_all(log_send, 'seq', split_axis=0, concat_axis=0, tiled=True)  5.55 us
    all_to_all x1, waiting for transfers between devices, on_device(): lax.all_to_all(delta_send, 'seq', split_axis=0, concat_axis=0, tiled=True)  5.04 us
    all_to_all x1, waiting for transfers between devices, on_device(): lax.all_to_all(keep_send, 'seq', split_axis=0, concat_axis=0, tiled=True)  4.34 us
  transfers between devices with their start and end apart: 14, of which 14 were waited for; matrix products, arithmetic and copies ran while one was open for 11% of the time, Pallas kernels for 0%

commit v1 on v0

v1 whole, which is shorter than its diff:
```python
import functools
import math

import jax
import jax.numpy as jnp
from jax import lax
from jax.experimental import pallas as pl
from jax.experimental.pallas import tpu as pltpu
from jax.sharding import PartitionSpec as P

CAP = 2
LOG2E = math.log2(math.e)
NT = (((1,), (1,)), ((), ()))
NN = (((1,), (0,)), ((), ()))


def kernel(
    heads, seqs, sel,
    owner_ref, q_ref, k_ref, v_ref, g_ref, o_ref, lm_ref,
    oq_ref, ok_ref, ov_ref,
    qh, gh, kh, vh, kt, dsend, dlt, lm, tab_f, tab_x, ret_ix,
    sqd, rqd, smeta, rmeta, dk, dv, gq, gk, gv, sret, ret,
    loc_sem, hs_sem, hr_sem, ds_sem, dr_sem, ms_sem, mr_sem, rs_sem, rr_sem, os_sem, or_sem,
):
    me_h = lax.axis_index("head")
    me_s = lax.axis_index("seq")
    cubes, rows, width = qh.shape
    piece = q_ref.shape[0]
    pairs = cubes * sel
    scale = 1.0 / math.sqrt(width)
    half = seqs // 2
    pow2 = seqs & (seqs - 1) == 0

    def goes_to(i):
        if not pow2:
            return (me_s + i) % seqs
        d = me_s
        for b in range(seqs.bit_length() - 1):
            w = 1 << b
            d = d + ((i // w) % 2) * w * (1 - 2 * ((me_s // w) % 2))
        return d

    def comes_from(i):
        return goes_to(i) if pow2 else (me_s + seqs - i) % seqs

    barrier = pltpu.get_barrier_semaphore()
    for t in range(1, heads):
        pl.semaphore_signal(barrier, inc=1, device_id={"head": (me_h + t) % heads, "seq": me_s})

    @pl.loop(1, seqs)
    def _(i):
        pl.semaphore_signal(barrier, inc=1, device_id={"head": me_h, "seq": goes_to(i)})

    def cols(h):
        return pl.ds(pl.multiple_of(h * width, width), width)

    def rows_of(h):
        return pl.ds(h * piece, piece)

    srcs = (q_ref, g_ref, k_ref, v_ref)
    dsts = (qh, gh, kh, vh)
    own = [
        pltpu.make_async_copy(s.at[:, :, cols(me_h)], d.at[rows_of(me_h)], loc_sem.at[n])
        for n, (s, d) in enumerate(zip(srcs, dsts))
    ]
    for c in own:
        c.start()

    for a in range(heads):
        for x in range(piece):
            prod = g_ref[x, :, a * width:(a + 1) * width].astype(jnp.float32) * o_ref[
                x, :, a * width:(a + 1) * width
            ].astype(jnp.float32)
            both = jnp.concatenate([prod] * CAP, axis=0)
            line = jnp.sum(both.T, axis=0, keepdims=True)
            dsend[a, x] = jnp.broadcast_to(line, (8, CAP * rows))

    lm[0:pairs] = lm_ref[...]
    lm[pairs] = jnp.full(lm.shape[1:], jnp.inf, jnp.float32)

    pl.semaphore_wait(barrier, heads - 1 + seqs - 1)

    head_copies = []
    for t in range(1, heads):
        to = (me_h + t) % heads
        for n, (s, d) in enumerate(zip(srcs, dsts)):
            head_copies.append((n, pltpu.make_async_remote_copy(
                src_ref=s.at[:, :, cols(to)], dst_ref=d.at[rows_of(me_h)],
                send_sem=hs_sem.at[t, n], recv_sem=hr_sem.at[t, n],
                device_id={"head": to, "seq": me_s})))
        head_copies.append((4, pltpu.make_async_remote_copy(
            src_ref=dsend.at[to], dst_ref=dlt.at[rows_of(me_h)],
            send_sem=hs_sem.at[t, 4], recv_sem=hr_sem.at[t, 4],
            device_id={"head": to, "seq": me_s})))
    for n in (0, 1, 4, 2, 3):
        for m, c in head_copies:
            if m == n:
                c.start()
    dlt[rows_of(me_h)] = dsend[me_h]

    @pl.loop(0, seqs)
    def _(d):
        count = jnp.int32(0)
        f = [jnp.int32(pairs)] * CAP
        xs = [jnp.int32(0)] * CAP
        for x in range(cubes):
            for j in range(sel):
                hit = owner_ref[x * sel + j] == d
                for c in range(CAP):
                    take = hit & (count == c)
                    f[c] = jnp.where(take, x * sel + j, f[c])
                    xs[c] = jnp.where(take, x, xs[c])
                count = count + hit.astype(jnp.int32)
        for c in range(CAP):
            tab_f[d * CAP + c] = f[c]
            tab_x[d * CAP + c] = xs[c]

    for c in own[:2]:
        c.wait()
    for m, c in head_copies:
        if m in (0, 1, 4):
            c.wait_recv()

    lane = lax.broadcasted_iota(jnp.int32, (8, CAP * rows), 1)

    def fill(d, slot, qd, meta):
        lines, deltas = None, None
        for c in range(CAP):
            x = tab_x[d * CAP + c]
            qd[slot, 0, c * rows:(c + 1) * rows] = qh[x]
            qd[slot, 1, c * rows:(c + 1) * rows] = gh[x]
            l_c, d_c = lm[tab_f[d * CAP + c]], dlt[x]
            lines = l_c if c == 0 else jnp.where(lane < c * rows, lines, l_c)
            deltas = d_c if c == 0 else jnp.where(lane < c * rows, deltas, d_c)
        meta[slot, 0:8] = lines
        meta[slot, 8:16] = deltas

    def data_copy(i, slot):
        dev = {"head": me_h, "seq": goes_to(i)}
        return (
            pltpu.make_async_remote_copy(
                src_ref=sqd.at[slot], dst_ref=rqd.at[slot], send_sem=ds_sem.at[slot],
                recv_sem=dr_sem.at[slot], device_id=dev),
            pltpu.make_async_remote_copy(
                src_ref=smeta.at[slot], dst_ref=rmeta.at[slot], send_sem=ms_sem.at[slot],
                recv_sem=mr_sem.at[slot], device_id=dev),
        )

    def back_copy(i, slot):
        return pltpu.make_async_remote_copy(
            src_ref=sret.at[slot], dst_ref=ret.at[pl.ds(me_s * CAP, CAP)],
            send_sem=rs_sem.at[slot], recv_sem=rr_sem.at[slot],
            device_id={"head": me_h, "seq": comes_from(i)})

    def send(i, slot):
        fill(goes_to(i), slot, sqd, smeta)
        for c in data_copy(i, slot):
            c.start()

    send(seqs - 1, 0)

    @pl.loop(1, half)
    def _(k):
        send(seqs - 1 - k, 2 * k)
        send(k, 2 * k + 1)

    fill(me_s, 1, rqd, rmeta)

    for c in own[2:]:
        c.wait()
    for m, c in head_copies:
        if m in (2, 3):
            c.wait_recv()

    keys = cubes * rows
    kt[...] = kh[...].reshape(keys, width).astype(jnp.float32).T.astype(jnp.bfloat16)
    dk[...] = jnp.zeros_like(dk)
    dv[...] = jnp.zeros_like(dv)
    wide = CAP * rows

    def work(k):
        base = 2 * k
        qb = jnp.concatenate([rqd[base, 0], rqd[base + 1, 0]], axis=0)
        gb = jnp.concatenate([rqd[base, 1], rqd[base + 1, 1]], axis=0)
        meta = jnp.concatenate([rmeta[base], rmeta[base + 1]], axis=1)
        kk = kh[...].reshape(keys, width)
        vv = vh[...].reshape(keys, width)
        st = lax.dot_general(kk, qb, NT, preferred_element_type=jnp.float32)
        dpt = lax.dot_general(vv, gb, NT, preferred_element_type=jnp.float32)
        st = st.reshape(cubes, rows, 2 * wide)
        p = jnp.exp2(st * (scale * LOG2E) - meta[0:8][:, None, :])
        ds = p * (dpt.reshape(cubes, rows, 2 * wide) - meta[8:9][:, None, :])
        pb = p.astype(jnp.bfloat16).reshape(keys, 2 * wide)
        dsb = ds.astype(jnp.bfloat16).reshape(keys, 2 * wide)
        dv[...] += lax.dot_general(pb, gb, NN, preferred_element_type=jnp.float32)
        dk[...] += lax.dot_general(dsb, qb, NN, preferred_element_type=jnp.float32)
        dqt = lax.dot_general(kt[...], dsb, NN, preferred_element_type=jnp.float32)
        dq = (dqt.T * scale).astype(jnp.bfloat16)
        return dq.reshape(2, CAP, rows, width)

    def arrive(i, slot):
        for c in data_copy(i, slot):
            c.wait_recv()

    arrive(seqs - 1, 0)
    dq = work(0)
    sret[0] = dq[0]
    back_copy(seqs - 1, 0).start()
    ret[pl.ds(me_s * CAP, CAP)] = dq[1]

    @pl.loop(1, half)
    def _(k):
        arrive(seqs - 1 - k, 2 * k)
        arrive(k, 2 * k + 1)
        dq = work(k)
        sret[2 * k] = dq[0]
        back_copy(seqs - 1 - k, 2 * k).start()
        sret[2 * k + 1] = dq[1]
        back_copy(k, 2 * k + 1).start()

    gk[...] = (dk[...] * scale).astype(jnp.bfloat16).reshape(gk.shape)
    gv[...] = dv[...].astype(jnp.bfloat16).reshape(gv.shape)
    grads, outs = (gk, gv, gq), (ok_ref, ov_ref, oq_ref)

    def out_copies(n):
        remote = []
        for t in range(1, heads):
            to = (me_h + t) % heads
            remote.append(pltpu.make_async_remote_copy(
                src_ref=grads[n].at[rows_of(to)], dst_ref=outs[n].at[:, :, cols(me_h)],
                send_sem=os_sem.at[t, n], recv_sem=or_sem.at[t, n],
                device_id={"head": to, "seq": me_s}))
        local = pltpu.make_async_copy(
            grads[n].at[rows_of(me_h)], outs[n].at[:, :, cols(me_h)], loc_sem.at[4 + n])
        return remote + [local]

    final = out_copies(0) + out_copies(1)
    for c in final:
        c.start()

    for x in range(cubes):
        for j in range(sel):
            d = owner_ref[x * sel + j]
            before = jnp.int32(0)
            for y in range(x):
                for m in range(sel):
                    before = before + (owner_ref[y * sel + m] == d).astype(jnp.int32)
            ret_ix[x * sel + j] = d * CAP + jnp.minimum(before, CAP - 1)

    back_copy(seqs - 1, 0).wait_recv()

    @pl.loop(1, half)
    def _(k):
        back_copy(seqs - 1 - k, 2 * k).wait_recv()
        back_copy(k, 2 * k + 1).wait_recv()

    for x in range(cubes):
        total = ret[ret_ix[x * sel]].astype(jnp.float32)
        for j in range(1, sel):
            total = total + ret[ret_ix[x * sel + j]].astype(jnp.float32)
        gq[x] = total.astype(jnp.bfloat16)
    last = out_copies(2)
    for c in last:
        c.start()

    for m, c in head_copies:
        c.wait_send()

    for c in data_copy(seqs - 1, 0):
        c.wait_send()
    back_copy(seqs - 1, 0).wait_send()

    @pl.loop(1, half)
    def _(k):
        for i, slot in ((seqs - 1 - k, 2 * k), (k, 2 * k + 1)):
            for c in data_copy(i, slot):
                c.wait_send()
            back_copy(i, slot).wait_send()

    for c in final + last:
        c.wait()


def on_device(
    query_rows, key_rows, value_rows, output_grad, output_rows, row_logsumexp,
    chosen_owner, chosen_cubes,
):
    heads = lax.axis_size("head")
    seqs = lax.axis_size("seq")
    piece_rows, full = query_rows.shape[2:]
    width = full // heads
    cubes, sel = chosen_owner.shape
    tokens = row_logsumexp.shape[0]
    rows = tokens // cubes
    piece = piece_rows // rows
    wide = CAP * rows

    def cubed(a):
        return a.reshape(piece, rows, full)

    log2 = row_logsumexp.reshape(cubes, rows) * LOG2E
    log2 = jnp.concatenate([log2] * CAP, axis=1)
    lm = jnp.where(
        chosen_cubes[:, :, :, None] != 0, log2[:, None, None, :], jnp.inf
    ).reshape(cubes * sel, cubes, wide)

    bf, f32, i32 = jnp.bfloat16, jnp.float32, jnp.int32
    vmem = pl.BlockSpec(memory_space=pltpu.VMEM)
    smem = pl.BlockSpec(memory_space=pltpu.SMEM)
    dma = pltpu.SemaphoreType.DMA
    tok = pltpu.VMEM((cubes, rows, width), bf)
    outs = pl.pallas_call(
        functools.partial(kernel, heads, seqs, sel),
        out_shape=[jax.ShapeDtypeStruct((piece, rows, full), bf)] * 3,
        in_specs=[smem] + [vmem] * 6,
        out_specs=[vmem] * 3,
        scratch_shapes=[
            tok, tok, tok, tok,
            pltpu.VMEM((width, cubes * rows), bf),
            pltpu.VMEM((heads, piece, 8, wide), f32),
            pltpu.VMEM((cubes, 8, wide), f32),
            pltpu.VMEM((cubes * sel + 1, 8, wide), f32),
            pltpu.SMEM((seqs * CAP,), i32),
            pltpu.SMEM((seqs * CAP,), i32),
            pltpu.SMEM((cubes * sel,), i32),
            pltpu.VMEM((seqs, 2, wide, width), bf),
            pltpu.VMEM((seqs, 2, wide, width), bf),
            pltpu.VMEM((seqs, 16, wide), f32),
            pltpu.VMEM((seqs, 16, wide), f32),
            pltpu.VMEM((cubes * rows, width), f32),
            pltpu.VMEM((cubes * rows, width), f32),
            tok, tok, tok,
            pltpu.VMEM((seqs, CAP, rows, width), bf),
            pltpu.VMEM((seqs * CAP, rows, width), bf),
            dma((7,)),
            dma((heads, 5)), dma((heads, 5)),
            dma((seqs,)), dma((seqs,)), dma((seqs,)), dma((seqs,)),
            dma((seqs,)), dma((seqs,)),
            dma((heads, 3)), dma((heads, 3)),
        ],
        compiler_params=pltpu.CompilerParams(collective_id=0, has_side_effects=True),
    )(
        chosen_owner.reshape(-1), cubed(query_rows), cubed(key_rows), cubed(value_rows),
        cubed(output_grad), cubed(output_rows), lm,
    )
    return tuple(a.reshape(1, 1, piece_rows, full) for a in outs)


def solution(mesh):
    rows = P("seq", "head", None, None)
    return jax.shard_map(
        on_device,
        mesh=mesh,
        in_specs=(rows, rows, rows, rows, rows, P("seq", "head"), P("seq", None), P("seq", None, None)),
        out_specs=(rows, rows, rows),
        check_vma=False,
    )
```

time: 177 us -> 62.2 us (0.35); the launches traced: 175 us -> 62 us
  waiting for transfers between devices: 86.9 us -> 0 us
  Pallas kernels: 0 us -> 55.2 us
  starting transfers between devices: 53.7 us -> 0 us
  local copies, waits for them, and re-layouts: 18.4 us -> 5.34 us
  matrix products: 10.1 us -> 0 us
  other arithmetic: 4.25 us -> 0.82 us
    all_to_all x14 -> x0, waiting for transfers between devices: 86.9 us -> none  [the longest x1 21.5 us: on_device(): lax.all_to_all(grad_q.reshape(seq_count, CAP, cube_rows, head_width), 'se...]
    pallas_call x0 -> x1, Pallas kernels: none -> 55.2 us  [on_device(): pl.pallas_call(functools.partial(kernel, heads, seqs, sel), out_shape=[ja...]
    all_to_all x14 -> x0, starting transfers between devices: 53.7 us -> none  [the longest x1 7.41 us: on_device(): lax.all_to_all(keep_send, 'seq', split_axis=0, concat_axis=0, tiled=True)]
    dot_general x27 -> x0, matrix products: 10.1 us -> none  [the longest x4 1.59 us: slot_step(): jnp.einsum('brk,brd->kd', dscores_low, query_part, preferred_element_type...]
    unnamed x35 -> x14, local copies, waits for them, and re-layouts: 10.7 us -> 4.64 us
    convert_element_type x4 -> x0, local copies, waits for them, and re-layouts: 2.38 us -> none  [the longest x1 0.93 us: on_device(): query_send = jnp.einsum('ncx,xrd->ncrd', table_low, query_cubes, preferre...]
    another operation x2 -> x0, local copies, waits for them, and re-layouts: 1.87 us -> none  [the longest x1 1.79 us: on_device(): grad_q.reshape(seq_count, CAP, cube_rows, head_width)]
  transfers between devices with their start and end apart: 14 -> 0, of which waited for: 14 -> 0; matrix products, arithmetic and copies ran while one was open for 11% -> 0% of each run, Pallas kernels for 0% -> 0%
where the time goes in v1:
time: 62.2 us; the launch traced here: 62 us
  Pallas kernels  55.2 us (89%)
  local copies, waits for them, and re-layouts  5.34 us (9%)
  other arithmetic  0.82 us (1%)
  between operations  0.67 us (1%)
    pallas_call x1, Pallas kernels, on_device(): pl.pallas_call(functools.partial(kernel, heads, seqs, sel), out_shape=[ja...  55.2 us
    unnamed x14, local copies, waits for them, and re-layouts  4.64 us

profile of v1, /device:TPU:0, one launch (start us, length us, event | category | flops | bytes accessed | tf_op | source)
XLA Modules:
  0.0 62.0 jit_solution(11927953678449640715)
XLA Ops:
  0.6 0.0 copy-start.3
  0.6 0.7 %copy-done.3 = f32[512,1]{0,1:T(1,128)S(1)} copy-done((f32[512,1]{0,1:T(1,128)S(1)}, f32[512,1]{0,1:T(1,128)}, u32[]{:S(2)}) %copy-start.3) | copy-done | bytes 2072
  1.3 0.1 mul.11
  1.4 0.1 pad_maximum_fusion
  1.5 0.0 copy-start.4
  1.5 0.0 copy-start.2
  1.5 0.7 %copy-done.4 = s32[8,2]{0,1:T(2,128)S(1)} copy-done((s32[8,2]{0,1:T(2,128)S(1)}, s32[8,2]{0,1:T(2,128)}, u32[]{:S(2)}) %copy-start.4) | copy-done | bytes 88
  2.2 0.1 copy.12
  2.2 0.6 reshape.43.owner_ref
  2.8 0.0 copy-done.2
  2.9 0.7 %broadcast_select_fusion.lm_ref = f32[16,8,128]{2,1,0:T(8,128)} fusion(f32[16,128]{1,0:T(8,128)S(1)} %bitcast.17, pred[16,8]{1,0:T(8,128)(4,1)S(1)} %broadcast_in_dim.28), kind=kLoop, calls=%fused_computation | loop fusion | flops 16384 | bytes 73856 | tf_op jit(solution)/shard_map/jit(_where)/select_n | solution.py:303
  3.6 55.2 %shard_map.103 = (bf16[4,64,256]{2,1,0:T(8,128)(2,1)}, bf16[4,64,256]{2,1,0:T(8,128)(2,1)}, bf16[4,64,256]{2,1,0:T(8,128)(2,1)}) custom-call(s32[16]{0:T(128)} %reshape.43.owner_ref, bf16[4,64,256]{2,1,0:T(8,128)(2,1)} %bitcast.9, bf16[4,64,256]{2,1,0:T(8,128)(2,1)} %bitcast.10, bf16[4,64,256]{2,1,0:T(8,128)(2,1)} %bitcast.11, bf16[4,64,256]{2,1,0:T(8,128)(2,1)} %bitcast.12, ...), custom_call_target="tpu_custom_call" | custom-call | tf_op jit(solution)/shard_map/pallas_call | solution.py:312
  58.8 0.0 copy-start.1
  58.8 1.6 %copy.16 = bf16[1,1,256,256]{3,2,1,0:T(8,128)(2,1)} copy(bf16[1,1,256,256]{3,2,1,0:T(8,128)(2,1)} %bitcast.16) | data formatting | bytes 262144
  60.4 0.0 copy-done.1
  60.4 0.0 copy-start
  60.4 0.7 %copy.17 = bf16[1,1,256,256]{3,2,1,0:T(8,128)(2,1)} copy(bf16[1,1,256,256]{3,2,1,0:T(8,128)(2,1)S(1)} %bitcast.15) | data formatting | bytes 262144
  61.0 0.3 copy-done
  61.3 0.7 %copy.18 = bf16[1,1,256,256]{3,2,1,0:T(8,128)(2,1)} copy(bf16[1,1,256,256]{3,2,1,0:T(8,128)(2,1)S(1)} %bitcast.14) | data formatting | bytes 262144
  (4 shorter events, 0.1 us)
Async XLA Ops:
  0.6 0.7 %copy-start.3 = (f32[512,1]{0,1:T(1,128)S(1)}, f32[512,1]{0,1:T(1,128)}, u32[]{:S(2)}) copy-start(f32[512,1]{0,1:T(1,128)} %param.13) | copy-start | bytes 6148
  1.5 0.7 %copy-start.4 = (s32[8,2]{0,1:T(2,128)S(1)}, s32[8,2]{0,1:T(2,128)}, u32[]{:S(2)}) copy-start(s32[8,2]{0,1:T(2,128)} %param.14) | copy-start | bytes 196
  1.5 1.3 %copy-start.2 = (s32[8,2,8]{2,1,0:T(2,128)S(1)}, s32[8,2,8]{2,1,0:T(2,128)}, u32[]{:S(2)}) copy-start(s32[8,2,8]{2,1,0:T(2,128)} %param.15) | copy-start | bytes 1540
  58.8 1.6 %copy-start.1 = (bf16[4,64,256]{2,1,0:T(8,128)(2,1)S(1)}, bf16[4,64,256]{2,1,0:T(8,128)(2,1)}, u32[]{:S(2)}) copy-start(bf16[4,64,256]{2,1,0:T(8,128)(2,1)} %get-tuple-element.7) | copy-start | bytes 393220
  60.4 1.0 %copy-start = (bf16[4,64,256]{2,1,0:T(8,128)(2,1)S(1)}, bf16[4,64,256]{2,1,0:T(8,128)(2,1)}, u32[]{:S(2)}) copy-start(bf16[4,64,256]{2,1,0:T(8,128)(2,1)} %get-tuple-element.8) | copy-start | bytes 393220

commit v2 on v1

v2 whole, which is shorter than its diff:
```python
import functools
import math

import jax
import jax.numpy as jnp
from jax import lax
from jax.experimental import pallas as pl
from jax.experimental.pallas import tpu as pltpu
from jax.sharding import PartitionSpec as P

CAP = 2
LOG2E = math.log2(math.e)
NT = (((1,), (1,)), ((), ()))
NN = (((1,), (0,)), ((), ()))


def kernel(
    heads, seqs, sel,
    owner_ref, table_ref, q_ref, k_ref, v_ref, g_ref, o_ref, lse_ref,
    oq_ref, ok_ref, ov_ref,
    qh, gh, kh, vh, kt, dsend, dlt, lz, tab_x, tab_m, ret_ix,
    fown, fown_s, fq, fg, fmeta, cmeta, ftab, fqd,
    sqd, rqd, smeta, rmeta, dk, dv, gq, gk, gv, sret, ret,
    loc_sem, hs_sem, hr_sem, xs_sem, xr_sem, ds_sem, dr_sem, ms_sem, mr_sem,
    rs_sem, rr_sem, os_sem, or_sem,
):
    me_h = lax.axis_index("head")
    me_s = lax.axis_index("seq")
    cubes, rows, width = qh.shape
    piece = q_ref.shape[0]
    pairs = cubes * sel
    scale = 1.0 / math.sqrt(width)
    half = seqs // 2
    wide = CAP * rows
    keys = cubes * rows
    metas = dlt.shape[1]

    def mate(i):
        d = me_s
        for b in range(seqs.bit_length() - 1):
            w = 1 << b
            d = d + ((i // w) % 2) * w * (1 - 2 * ((me_s // w) % 2))
        return d

    far = mate(half)

    barrier = pltpu.get_barrier_semaphore()
    for t in range(1, heads):
        pl.semaphore_signal(barrier, inc=1, device_id={"head": (me_h + t) % heads, "seq": me_s})

    @pl.loop(1, seqs)
    def _(i):
        pl.semaphore_signal(barrier, inc=1, device_id={"head": me_h, "seq": mate(i)})

    def cols(h):
        return pl.ds(pl.multiple_of(h * width, width), width)

    def rows_of(h):
        return pl.ds(h * piece, piece)

    srcs = (q_ref, g_ref, k_ref, v_ref)
    dsts = (qh, gh, kh, vh)
    own = [
        pltpu.make_async_copy(s.at[:, :, cols(me_h)], d.at[rows_of(me_h)], loc_sem.at[n])
        for n, (s, d) in enumerate(zip(srcs, dsts))
    ]
    for c in own:
        c.start()

    row = lax.broadcasted_iota(jnp.int32, (metas, wide), 0)
    lane = lax.broadcasted_iota(jnp.int32, (metas, wide), 1)
    for a in range(heads):
        for x in range(piece):
            prod = g_ref[x, :, a * width:(a + 1) * width].astype(jnp.float32) * o_ref[
                x, :, a * width:(a + 1) * width
            ].astype(jnp.float32)
            both = jnp.concatenate([prod] * CAP, axis=0)
            line = jnp.sum(both.T, axis=0, keepdims=True)
            dsend[a, x] = jnp.where(row == 1, jnp.broadcast_to(line, (metas, wide)), 0.0)
    for x in range(cubes):
        line = jnp.concatenate([lse_ref[:, x * rows:(x + 1) * rows] * LOG2E] * CAP, axis=1)
        lz[x] = jnp.where(row == 0, jnp.broadcast_to(line, (metas, wide)), 0.0)

    pl.semaphore_wait(barrier, heads - 1 + seqs - 1)

    def head_copy(t, n):
        to = (me_h + t) % heads
        if n == 4:
            src, dst = dsend.at[to], dlt.at[rows_of(me_h)]
        else:
            src, dst = srcs[n].at[:, :, cols(to)], dsts[n].at[rows_of(me_h)]
        return pltpu.make_async_remote_copy(
            src_ref=src, dst_ref=dst, send_sem=hs_sem.at[t, n], recv_sem=hr_sem.at[t, n],
            device_id={"head": to, "seq": me_s})

    def far_copy(n, src, dst):
        return pltpu.make_async_remote_copy(
            src_ref=src, dst_ref=dst, send_sem=xs_sem.at[n], recv_sem=xr_sem.at[n],
            device_id={"head": me_h, "seq": far})

    def far_part(n, t):
        h = (me_h + heads - t) % heads
        src = srcs[n].at[:, :, cols(me_h)] if t == 0 else dsts[n].at[rows_of(h)]
        return far_copy(2 + n * heads + t, src, (fq, fg)[n].at[rows_of(h)])

    owners = far_copy(0, table_ref, fown)
    far_meta = far_copy(1, cmeta, fmeta)

    owners.start()
    far_part(0, 0).start()
    for n in (0, 1, 4, 2, 3):
        for t in range(1, heads):
            head_copy(t, n).start()
    dlt[rows_of(me_h)] = dsend[me_h]

    def slots_of(read, d):
        count = jnp.int32(0)
        xs = [jnp.int32(0)] * CAP
        fs = [jnp.int32(-1)] * CAP
        for x in range(cubes):
            for j in range(sel):
                hit = read(x * sel + j) == d
                for c in range(CAP):
                    take = hit & (count == c)
                    xs[c] = jnp.where(take, x, xs[c])
                    fs[c] = jnp.where(take, x * sel + j, fs[c])
                count = count + hit.astype(jnp.int32)
        return xs, fs

    @pl.loop(0, seqs)
    def _(i):
        xs, fs = slots_of(lambda f: owner_ref[f], mate(i))
        for c in range(CAP):
            bits = owner_ref[pairs + jnp.maximum(fs[c], 0)]
            tab_x[i * CAP + c] = xs[c]
            tab_m[i * CAP + c] = jnp.where(fs[c] >= 0, bits, 0)

    for t in range(1, heads):
        head_copy(t, 0).wait_recv()
        far_part(0, t).start()
    far_part(1, 0).start()
    for t in range(1, heads):
        head_copy(t, 1).wait_recv()
        far_part(1, t).start()
    for c in own[:2]:
        c.wait()
    for t in range(1, heads):
        head_copy(t, 4).wait_recv()

    def info(i):
        both = None
        for c in range(CAP):
            x = tab_x[i * CAP + c]
            bits = tab_m[i * CAP + c].astype(jnp.float32)
            one = jnp.where(row == 2, bits, dlt[x] + lz[x])
            both = one if c == 0 else jnp.where(lane < c * rows, both, one)
        return both

    @pl.loop(0, half)
    def _(i):
        cmeta[i] = info(half + i)

    far_meta.start()

    def data_copy(i):
        dev = {"head": me_h, "seq": mate(i)}
        return (
            pltpu.make_async_remote_copy(
                src_ref=sqd.at[i], dst_ref=rqd.at[i], send_sem=ds_sem.at[i],
                recv_sem=dr_sem.at[i], device_id=dev),
            pltpu.make_async_remote_copy(
                src_ref=smeta.at[i], dst_ref=rmeta.at[i], send_sem=ms_sem.at[i],
                recv_sem=mr_sem.at[i], device_id=dev),
        )

    def passed_copy(i, n):
        dev = {"head": me_h, "seq": mate(i)}
        if n == 2:
            return pltpu.make_async_remote_copy(
                src_ref=fmeta.at[i], dst_ref=rmeta.at[half + i], send_sem=ms_sem.at[half + i],
                recv_sem=mr_sem.at[half + i], device_id=dev)
        return pltpu.make_async_remote_copy(
            src_ref=fqd.at[i, n], dst_ref=rqd.at[half + i, n],
            send_sem=ds_sem.at[half + i + n * half],
            recv_sem=dr_sem.at[half + i + n * half], device_id=dev)

    def back_copy(i):
        return pltpu.make_async_remote_copy(
            src_ref=sret.at[i], dst_ref=ret.at[pl.ds(me_s * CAP, CAP)],
            send_sem=rs_sem.at[i], recv_sem=rr_sem.at[i],
            device_id={"head": me_h, "seq": mate(i)})

    def fill(i, qd, meta):
        for c in range(CAP):
            x = tab_x[i * CAP + c]
            qd[i, 0, c * rows:(c + 1) * rows] = qh[x]
            qd[i, 1, c * rows:(c + 1) * rows] = gh[x]
        meta[i] = info(i)

    @pl.loop(1, half)
    def _(i):
        fill(half - i, sqd, smeta)
        for c in data_copy(half - i):
            c.start()

    fill(0, rqd, rmeta)

    owners.wait_recv()
    to_smem = pltpu.make_async_copy(fown, fown_s, loc_sem.at[7])
    to_smem.start()
    to_smem.wait()

    @pl.loop(0, half)
    def _(i):
        xs, _ = slots_of(lambda f: fown_s[0, f], mate(i))
        for c in range(CAP):
            ftab[i * CAP + c] = xs[c]

    def pass_on(n):
        src = (fq, fg)[n]
        for t in range(heads):
            far_part(n, t).wait_recv()

        @pl.loop(1, half)
        def _(k):
            i = half - k
            for c in range(CAP):
                fqd[i, n, c * rows:(c + 1) * rows] = src[ftab[i * CAP + c]]
            passed_copy(i, n).start()

        for c in range(CAP):
            rqd[half, n, c * rows:(c + 1) * rows] = src[ftab[c]]

    pass_on(0)
    far_meta.wait_recv()

    @pl.loop(1, half)
    def _(i):
        passed_copy(i, 2).start()

    rmeta[half] = fmeta[0]

    for c in own[2:]:
        c.wait()
    for t in range(1, heads):
        head_copy(t, 2).wait_recv()
        head_copy(t, 3).wait_recv()

    kt[...] = kh[...].reshape(keys, width).astype(jnp.float32).T.astype(jnp.bfloat16)
    dk[...] = jnp.zeros_like(dk)
    dv[...] = jnp.zeros_like(dv)
    bit = lax.broadcasted_iota(jnp.int32, (cubes, 2 * wide), 0)

    def work(k):
        base = 2 * k
        qb = jnp.concatenate([rqd[base, 0], rqd[base + 1, 0]], axis=0)
        gb = jnp.concatenate([rqd[base, 1], rqd[base + 1, 1]], axis=0)
        meta = jnp.concatenate([rmeta[base], rmeta[base + 1]], axis=1)
        kept = (meta[2:3].astype(jnp.int32) >> bit) & 1
        line = jnp.where(kept == 1, meta[0:1], jnp.inf)
        kk = kh[...].reshape(keys, width)
        vv = vh[...].reshape(keys, width)
        st = lax.dot_general(kk, qb, NT, preferred_element_type=jnp.float32)
        dpt = lax.dot_general(vv, gb, NT, preferred_element_type=jnp.float32)
        st = st.reshape(cubes, rows, 2 * wide)
        p = jnp.exp2(st * (scale * LOG2E) - line[:, None, :])
        ds = p * (dpt.reshape(cubes, rows, 2 * wide) - meta[1:2][:, None, :])
        pb = p.astype(jnp.bfloat16).reshape(keys, 2 * wide)
        dsb = ds.astype(jnp.bfloat16).reshape(keys, 2 * wide)
        dv[...] += lax.dot_general(pb, gb, NN, preferred_element_type=jnp.float32)
        dk[...] += lax.dot_general(dsb, qb, NN, preferred_element_type=jnp.float32)
        dqt = lax.dot_general(kt[...], dsb, NN, preferred_element_type=jnp.float32)
        dq = (dqt.T * scale).astype(jnp.bfloat16)
        return dq.reshape(2, CAP, rows, width)

    def near_in(i):
        for c in data_copy(i):
            c.wait_recv()

    def far_in(i):
        for n in range(3):
            passed_copy(i, n).wait_recv()

    def give(i, dq):
        sret[i] = dq
        back_copy(i).start()

    near_in(1)
    dq = work(0)
    ret[pl.ds(me_s * CAP, CAP)] = dq[0]
    give(1, dq[1])

    @pl.loop(1, half // 2)
    def _(k):
        near_in(2 * k)
        near_in(2 * k + 1)
        dq = work(k)
        give(2 * k, dq[0])
        give(2 * k + 1, dq[1])

    pass_on(1)

    far_in(1)
    dq = work(half // 2)
    give(half, dq[0])
    give(half + 1, dq[1])

    @pl.loop(1, half // 2)
    def _(k):
        far_in(2 * k)
        far_in(2 * k + 1)
        dq = work(half // 2 + k)
        give(half + 2 * k, dq[0])
        give(half + 2 * k + 1, dq[1])

    gk[...] = (dk[...] * scale).astype(jnp.bfloat16).reshape(gk.shape)
    gv[...] = dv[...].astype(jnp.bfloat16).reshape(gv.shape)
    grads, outs = (gk, gv, gq), (ok_ref, ov_ref, oq_ref)

    def out_copies(n):
        remote = []
        for t in range(1, heads):
            to = (me_h + t) % heads
            remote.append(pltpu.make_async_remote_copy(
                src_ref=grads[n].at[rows_of(to)], dst_ref=outs[n].at[:, :, cols(me_h)],
                send_sem=os_sem.at[t, n], recv_sem=or_sem.at[t, n],
                device_id={"head": to, "seq": me_s}))
        local = pltpu.make_async_copy(
            grads[n].at[rows_of(me_h)], outs[n].at[:, :, cols(me_h)], loc_sem.at[4 + n])
        return remote + [local]

    final = out_copies(0) + out_copies(1)
    for c in final:
        c.start()

    for x in range(cubes):
        for j in range(sel):
            d = owner_ref[x * sel + j]
            before = jnp.int32(0)
            for y in range(x):
                for m in range(sel):
                    before = before + (owner_ref[y * sel + m] == d).astype(jnp.int32)
            ret_ix[x * sel + j] = d * CAP + jnp.minimum(before, CAP - 1)

    @pl.loop(1, seqs)
    def _(i):
        back_copy(i).wait_recv()

    for x in range(cubes):
        total = ret[ret_ix[x * sel]].astype(jnp.float32)
        for j in range(1, sel):
            total = total + ret[ret_ix[x * sel + j]].astype(jnp.float32)
        gq[x] = total.astype(jnp.bfloat16)
    last = out_copies(2)
    for c in last:
        c.start()

    for t in range(1, heads):
        for n in range(5):
            head_copy(t, n).wait_send()
    owners.wait_send()
    far_meta.wait_send()
    for n in range(2):
        for t in range(heads):
            far_part(n, t).wait_send()

    @pl.loop(1, half)
    def _(i):
        for c in data_copy(i):
            c.wait_send()
        for n in range(3):
            passed_copy(i, n).wait_send()

    @pl.loop(1, seqs)
    def _(i):
        back_copy(i).wait_send()

    for c in final + last:
        c.wait()


def on_device(
    query_rows, key_rows, value_rows, output_grad, output_rows, row_logsumexp,
    chosen_owner, chosen_cubes,
):
    heads = lax.axis_size("head")
    seqs = lax.axis_size("seq")
    piece_rows, full = query_rows.shape[2:]
    width = full // heads
    cubes, sel = chosen_owner.shape
    tokens = row_logsumexp.shape[0]
    rows = tokens // cubes
    piece = piece_rows // rows
    wide = CAP * rows
    half = seqs // 2

    def cubed(a):
        return a.reshape(piece, rows, full)

    weight = 1 << jnp.arange(chosen_cubes.shape[2], dtype=jnp.int32)
    bits = jnp.sum(jnp.where(chosen_cubes != 0, weight, 0), axis=2)
    table = jnp.stack([chosen_owner, bits]).reshape(-1)
    lanes = -(-chosen_owner.size // 128) * 128
    owners = jnp.pad(chosen_owner.reshape(1, -1), ((0, 0), (0, lanes - chosen_owner.size)))

    bf, f32, i32 = jnp.bfloat16, jnp.float32, jnp.int32
    vmem = pl.BlockSpec(memory_space=pltpu.VMEM)
    smem = pl.BlockSpec(memory_space=pltpu.SMEM)
    dma = pltpu.SemaphoreType.DMA
    tok = pltpu.VMEM((cubes, rows, width), bf)
    outs = pl.pallas_call(
        functools.partial(kernel, heads, seqs, sel),
        out_shape=[jax.ShapeDtypeStruct((piece, rows, full), bf)] * 3,
        in_specs=[smem] + [vmem] * 7,
        out_specs=[vmem] * 3,
        scratch_shapes=[
            tok, tok, tok, tok,
            pltpu.VMEM((width, cubes * rows), bf),
            pltpu.VMEM((heads, piece, 4, wide), f32),
            pltpu.VMEM((cubes, 4, wide), f32),
            pltpu.VMEM((cubes, 4, wide), f32),
            pltpu.SMEM((seqs * CAP,), i32),
            pltpu.SMEM((seqs * CAP,), i32),
            pltpu.SMEM((cubes * sel,), i32),
            pltpu.VMEM((1, lanes), i32),
            pltpu.SMEM((1, lanes), i32),
            tok, tok,
            pltpu.VMEM((half, 4, wide), f32),
            pltpu.VMEM((half, 4, wide), f32),
            pltpu.SMEM((half * CAP,), i32),
            pltpu.VMEM((half, 2, wide, width), bf),
            pltpu.VMEM((half, 2, wide, width), bf),
            pltpu.VMEM((seqs, 2, wide, width), bf),
            pltpu.VMEM((half, 4, wide), f32),
            pltpu.VMEM((seqs, 4, wide), f32),
            pltpu.VMEM((cubes * rows, width), f32),
            pltpu.VMEM((cubes * rows, width), f32),
            tok, tok, tok,
            pltpu.VMEM((seqs, CAP, rows, width), bf),
            pltpu.VMEM((seqs * CAP, rows, width), bf),
            dma((8,)),
            dma((heads, 5)), dma((heads, 5)),
            dma((2 + 2 * heads,)), dma((2 + 2 * heads,)),
            dma((seqs + half,)), dma((seqs + half,)), dma((seqs,)), dma((seqs,)),
            dma((seqs,)), dma((seqs,)),
            dma((heads, 3)), dma((heads, 3)),
        ],
        compiler_params=pltpu.CompilerParams(collective_id=0, has_side_effects=True),
    )(
        table, owners, cubed(query_rows), cubed(key_rows), cubed(value_rows),
        cubed(output_grad), cubed(output_rows),
        row_logsumexp.reshape(1, tokens),
    )
    return tuple(a.reshape(1, 1, piece_rows, full) for a in outs)


def solution(mesh):
    rows = P("seq", "head", None, None)
    return jax.shard_map(
        on_device,
        mesh=mesh,
        in_specs=(rows, rows, rows, rows, rows, P("seq", "head"), P("seq", None), P("seq", None, None)),
        out_specs=(rows, rows, rows),
        check_vma=False,
    )
```

time: 62.2 us -> 52.4 us (0.84)
  Pallas kernels: 55.2 us -> 45 us
  local copies, waits for them, and re-layouts: 5.34 us -> 6.03 us
    pallas_call x1, Pallas kernels: 55.2 us -> 45 us  [on_device(): pl.pallas_call(functools.partial(kernel, heads, seqs, sel), out_shape=[ja...]
    select_n x1 -> x0, other arithmetic: 0.72 us -> none  [on_device(): jnp.where(chosen_cubes[:, :, :, None] != 0, log2[:, None, None, :], jnp.inf)]
    unnamed x14 -> x12, local copies, waits for them, and re-layouts: 4.64 us -> 4.66 us
where the time goes in v2:
time: 52.4 us; the launch traced here: 51.9 us
  Pallas kernels  45 us (86%)
  local copies, waits for them, and re-layouts  6.03 us (12%)
  between operations  0.67 us (1%)
    pallas_call x1, Pallas kernels, on_device(): pl.pallas_call(functools.partial(kernel, heads, seqs, sel), out_shape=[ja...  45 us
    unnamed x12, local copies, waits for them, and re-layouts  4.66 us

profile of v2, /device:TPU:0, one launch (start us, length us, event | category | flops | bytes accessed | tf_op | source)
XLA Modules:
  0.0 51.9 jit_solution(13507124163136963320)
XLA Ops:
  0.6 0.0 copy-start.2
  0.7 0.7 %copy-done.2 = s32[8,2,8]{2,1,0:T(2,128)S(1)} copy-done((s32[8,2,8]{2,1,0:T(2,128)S(1)}, s32[8,2,8]{2,1,0:T(2,128)}, u32[]{:S(2)}) %copy-start.2) | copy-done | bytes 536
  1.3 0.2 fusion
  1.5 0.1 copy.15
  1.6 0.0 copy-start.3
  1.6 0.7 %copy-done.3 = s32[8,2]{0,1:T(2,128)S(1)} copy-done((s32[8,2]{0,1:T(2,128)S(1)}, s32[8,2]{0,1:T(2,128)}, u32[]{:S(2)}) %copy-start.3) | copy-done | bytes 88
  2.3 0.1 copy.17
  2.4 0.1 reshape.40
  2.5 0.5 %pad.4.table_ref = s32[1,128]{1,0:T(1,128)} pad(s32[1,16]{1,0:T(1,128)S(1)} %reshape.40, s32[]{:T(128)} %constant.2.clone.1), padding=0_0x0_112 | pad | bytes 580 | tf_op jit(solution)/shard_map/jit(_pad)/pad | solution.py:404
  3.0 0.1 copy.16
  3.1 0.6 %reshape.39.owner_ref = s32[32]{0:T(128)} reshape(s32[2,8,2]{2,1,0:T(8,128)S(1)} %copy.16) | data formatting | bytes 256 | tf_op jit(solution)/shard_map/reshape | solution.py:402
  3.7 45.0 %shard_map.103 = (bf16[4,64,256]{2,1,0:T(8,128)(2,1)}, bf16[4,64,256]{2,1,0:T(8,128)(2,1)}, bf16[4,64,256]{2,1,0:T(8,128)(2,1)}) custom-call(s32[32]{0:T(128)} %reshape.39.owner_ref, s32[1,128]{1,0:T(1,128)} %pad.4.table_ref, bf16[4,64,256]{2,1,0:T(8,128)(2,1)} %bitcast.11, bf16[4,64,256]{2,1,0:T(8,128)(2,1)} %bitcast.12, bf16[4,64,256]{2,1,0:T(8,128)(2,1)} %bitcast.13, ...), custom_call_target="tpu_custom_call" | custom-call | tf_op jit(solution)/shard_map/pallas_call | solution.py:411
  48.7 0.0 copy-start.1
  48.7 1.6 %copy.21 = bf16[1,1,256,256]{3,2,1,0:T(8,128)(2,1)} copy(bf16[1,1,256,256]{3,2,1,0:T(8,128)(2,1)} %bitcast.18) | data formatting | bytes 262144
  50.3 0.0 copy-done.1
  50.3 0.0 copy-start
  50.3 0.7 %copy.22 = bf16[1,1,256,256]{3,2,1,0:T(8,128)(2,1)} copy(bf16[1,1,256,256]{3,2,1,0:T(8,128)(2,1)S(1)} %bitcast.17) | data formatting | bytes 262144
  51.0 0.3 copy-done
  51.3 0.7 %copy.23 = bf16[1,1,256,256]{3,2,1,0:T(8,128)(2,1)} copy(bf16[1,1,256,256]{3,2,1,0:T(8,128)(2,1)S(1)} %bitcast.16) | data formatting | bytes 262144
  (2 shorter events, 0.0 us)
Async XLA Ops:
  0.6 0.7 %copy-start.2 = (s32[8,2,8]{2,1,0:T(2,128)S(1)}, s32[8,2,8]{2,1,0:T(2,128)}, u32[]{:S(2)}) copy-start(s32[8,2,8]{2,1,0:T(2,128)} %param.15) | copy-start | bytes 1540
  1.6 0.7 %copy-start.3 = (s32[8,2]{0,1:T(2,128)S(1)}, s32[8,2]{0,1:T(2,128)}, u32[]{:S(2)}) copy-start(s32[8,2]{0,1:T(2,128)} %param.14) | copy-start | bytes 196
  48.7 1.6 %copy-start.1 = (bf16[4,64,256]{2,1,0:T(8,128)(2,1)S(1)}, bf16[4,64,256]{2,1,0:T(8,128)(2,1)}, u32[]{:S(2)}) copy-start(bf16[4,64,256]{2,1,0:T(8,128)(2,1)} %get-tuple-element.7) | copy-start | bytes 393220
  50.3 1.0 %copy-start = (bf16[4,64,256]{2,1,0:T(8,128)(2,1)S(1)}, bf16[4,64,256]{2,1,0:T(8,128)(2,1)}, u32[]{:S(2)}) copy-start(bf16[4,64,256]{2,1,0:T(8,128)(2,1)} %get-tuple-element.8) | copy-start | bytes 393220

commit v3 on v2

--- a/solution.py
+++ b/solution.py
@@ -16,9 +16,9 @@
 
 def kernel(
     heads, seqs, sel,
-    owner_ref, table_ref, q_ref, k_ref, v_ref, g_ref, o_ref, lse_ref,
+    owner_ref, pick_ref, table_ref, q_ref, k_ref, v_ref, g_ref, o_ref, lse_ref,
     oq_ref, ok_ref, ov_ref,
-    qh, gh, kh, vh, kt, dsend, dlt, lz, tab_x, tab_m, ret_ix,
+    qh, gh, kh, vh, kt, g_all, o_all, dsend, dlt, lz, bits_of, tab_x, tab_m, ret_ix,
     fown, fown_s, fq, fg, fmeta, cmeta, ftab, fqd,
     sqd, rqd, smeta, rmeta, dk, dv, gq, gk, gv, sret, ret,
     loc_sem, hs_sem, hr_sem, xs_sem, xr_sem, ds_sem, dr_sem, ms_sem, mr_sem,
@@ -28,7 +28,6 @@
     me_s = lax.axis_index("seq")
     cubes, rows, width = qh.shape
     piece = q_ref.shape[0]
-    pairs = cubes * sel
     scale = 1.0 / math.sqrt(width)
     half = seqs // 2
     wide = CAP * rows
@@ -64,14 +63,28 @@
         pltpu.make_async_copy(s.at[:, :, cols(me_h)], d.at[rows_of(me_h)], loc_sem.at[n])
         for n, (s, d) in enumerate(zip(srcs, dsts))
     ]
-    for c in own:
+    whole = [
+        pltpu.make_async_copy(s, d, loc_sem.at[8 + n])
+        for n, (s, d) in enumerate(((g_ref, g_all), (o_ref, o_all)))
+    ]
+    for c in whole + own:
         c.start()
+
+    for x in range(cubes):
+        for j in range(sel):
+            bits = jnp.int32(0)
+            for k in range(cubes):
+                bits = bits + jnp.where(pick_ref[x, j, k] != 0, 1 << k, 0)
+            bits_of[x * sel + j] = bits
+
+    for c in whole:
+        c.wait()
 
     row = lax.broadcasted_iota(jnp.int32, (metas, wide), 0)
     lane = lax.broadcasted_iota(jnp.int32, (metas, wide), 1)
     for a in range(heads):
         for x in range(piece):
-            prod = g_ref[x, :, a * width:(a + 1) * width].astype(jnp.float32) * o_ref[
+            prod = g_all[x, :, a * width:(a + 1) * width].astype(jnp.float32) * o_all[
                 x, :, a * width:(a + 1) * width
             ].astype(jnp.float32)
             both = jnp.concatenate([prod] * CAP, axis=0)
@@ -119,7 +132,7 @@
         fs = [jnp.int32(-1)] * CAP
         for x in range(cubes):
             for j in range(sel):
-                hit = read(x * sel + j) == d
+                hit = read(x, j) == d
                 for c in range(CAP):
                     take = hit & (count == c)
                     xs[c] = jnp.where(take, x, xs[c])
@@ -129,9 +142,9 @@
 
     @pl.loop(0, seqs)
     def _(i):
-        xs, fs = slots_of(lambda f: owner_ref[f], mate(i))
+        xs, fs = slots_of(lambda x, j: owner_ref[j, x], mate(i))
         for c in range(CAP):
-            bits = owner_ref[pairs + jnp.maximum(fs[c], 0)]
+            bits = bits_of[jnp.maximum(fs[c], 0)]
             tab_x[i * CAP + c] = xs[c]
             tab_m[i * CAP + c] = jnp.where(fs[c] >= 0, bits, 0)
 
@@ -212,7 +225,7 @@
 
     @pl.loop(0, half)
     def _(i):
-        xs, _ = slots_of(lambda f: fown_s[0, f], mate(i))
+        xs, _ = slots_of(lambda x, j: fown_s[j, x], mate(i))
         for c in range(CAP):
             ftab[i * CAP + c] = xs[c]
 
@@ -335,11 +348,11 @@
 
     for x in range(cubes):
         for j in range(sel):
-            d = owner_ref[x * sel + j]
+            d = owner_ref[j, x]
             before = jnp.int32(0)
             for y in range(x):
                 for m in range(sel):
-                    before = before + (owner_ref[y * sel + m] == d).astype(jnp.int32)
+                    before = before + (owner_ref[m, y] == d).astype(jnp.int32)
             ret_ix[x * sel + j] = d * CAP + jnp.minimum(before, CAP - 1)
 
     @pl.loop(1, seqs)
@@ -376,6 +389,17 @@
         back_copy(i).wait_send()
 
     for c in final + last:
+        c.wait()
+
+
+def place(a_ref, b_ref, c_ref, x_ref, y_ref, z_ref, sem):
+    copies = [
+        pltpu.make_async_copy(s, d, sem.at[n])
+        for n, (s, d) in enumerate(((a_ref, x_ref), (b_ref, y_ref), (c_ref, z_ref)))
+    ]
+    for c in copies:
+        c.start()
+    for c in copies:
         c.wait()
 
 
@@ -397,33 +421,31 @@
     def cubed(a):
         return a.reshape(piece, rows, full)
 
-    weight = 1 << jnp.arange(chosen_cubes.shape[2], dtype=jnp.int32)
-    bits = jnp.sum(jnp.where(chosen_cubes != 0, weight, 0), axis=2)
-    table = jnp.stack([chosen_owner, bits]).reshape(-1)
-    lanes = -(-chosen_owner.size // 128) * 128
-    owners = jnp.pad(chosen_owner.reshape(1, -1), ((0, 0), (0, lanes - chosen_owner.size)))
-
     bf, f32, i32 = jnp.bfloat16, jnp.float32, jnp.int32
     vmem = pl.BlockSpec(memory_space=pltpu.VMEM)
+    anywhere = pl.BlockSpec(memory_space=pl.ANY)
     smem = pl.BlockSpec(memory_space=pltpu.SMEM)
     dma = pltpu.SemaphoreType.DMA
     tok = pltpu.VMEM((cubes, rows, width), bf)
     outs = pl.pallas_call(
         functools.partial(kernel, heads, seqs, sel),
         out_shape=[jax.ShapeDtypeStruct((piece, rows, full), bf)] * 3,
-        in_specs=[smem] + [vmem] * 7,
-        out_specs=[vmem] * 3,
+        in_specs=[smem, smem, vmem] + [anywhere] * 5 + [vmem],
+        out_specs=[anywhere] * 3,
         scratch_shapes=[
             tok, tok, tok, tok,
             pltpu.VMEM((width, cubes * rows), bf),
+            pltpu.VMEM((piece, rows, full), bf),
+            pltpu.VMEM((piece, rows, full), bf),
             pltpu.VMEM((heads, piece, 4, wide), f32),
             pltpu.VMEM((cubes, 4, wide), f32),
             pltpu.VMEM((cubes, 4, wide), f32),
+            pltpu.SMEM((cubes * sel,), i32),
             pltpu.SMEM((seqs * CAP,), i32),
             pltpu.SMEM((seqs * CAP,), i32),
             pltpu.SMEM((cubes * sel,), i32),
-            pltpu.VMEM((1, lanes), i32),
-            pltpu.SMEM((1, lanes), i32),
+            pltpu.VMEM((sel, cubes), i32),
+            pltpu.SMEM((sel, cubes), i32),
             tok, tok,
             pltpu.VMEM((half, 4, wide), f32),
             pltpu.VMEM((half, 4, wide), f32),
@@ -438,7 +460,7 @@
             tok, tok, tok,
             pltpu.VMEM((seqs, CAP, rows, width), bf),
             pltpu.VMEM((seqs * CAP, rows, width), bf),
-            dma((8,)),
+            dma((10,)),
             dma((heads, 5)), dma((heads, 5)),
             dma((2 + 2 * heads,)), dma((2 + 2 * heads,)),
             dma((seqs + half,)), dma((seqs + half,)), dma((seqs,)), dma((seqs,)),
@@ -447,10 +469,17 @@
         ],
         compiler_params=pltpu.CompilerParams(collective_id=0, has_side_effects=True),
     )(
-        table, owners, cubed(query_rows), cubed(key_rows), cubed(value_rows),
+        chosen_owner.T, chosen_cubes, chosen_owner.T, cubed(query_rows), cubed(key_rows), cubed(value_rows),
         cubed(output_grad), cubed(output_rows),
         row_logsumexp.reshape(1, tokens),
     )
+    outs = pl.pallas_call(
+        place,
+        out_shape=[jax.ShapeDtypeStruct((piece, rows, full), bf)] * 3,
+        in_specs=[anywhere] * 3,
+        out_specs=[vmem] * 3,
+        scratch_shapes=[dma((3,))],
+    )(*outs)
     return tuple(a.reshape(1, 1, piece_rows, full) for a in outs)
 
 

time: 52.4 us -> 47.3 us (0.903)
  local copies, waits for them, and re-layouts: 6.03 us -> 0 us
  Pallas kernels: 45 us -> 46.4 us
    unnamed x12 -> x0, local copies, waits for them, and re-layouts: 4.66 us -> none
    pallas_call x0 -> x1, Pallas kernels: none -> 1.8 us  [on_device(): pl.pallas_call(place, out_shape=[jax.ShapeDtypeStruct((piece, rows, full)...]
    reshape x2 -> x0, local copies, waits for them, and re-layouts: 0.68 us -> none  [the longest x1 0.6 us: on_device(): table = jnp.stack([chosen_owner, bits]).reshape(-1)]
where the time goes in v3:
time: 47.3 us; the launch traced here: 47.1 us
  Pallas kernels  46.4 us (98%)
  between operations  0.64 us (1%)
    pallas_call x1, Pallas kernels, on_device(): pl.pallas_call(functools.partial(kernel, heads, seqs, sel), out_shape=[ja...  44.6 us
    pallas_call x1, Pallas kernels, on_device(): pl.pallas_call(place, out_shape=[jax.ShapeDtypeStruct((piece, rows, full)...  1.8 us

profile of v3, /device:TPU:0, one launch (start us, length us, event | category | flops | bytes accessed | tf_op | source)
XLA Modules:
  0.0 47.1 jit_solution(14191317756421346743)
XLA Ops:
  0.6 44.6 %shard_map.103 = (bf16[4,64,256]{2,1,0:T(8,128)(2,1)}, bf16[4,64,256]{2,1,0:T(8,128)(2,1)}, bf16[4,64,256]{2,1,0:T(8,128)(2,1)}) custom-call(s32[2,8]{1,0:T(2,128)} %bitcast.15, s32[8,2,8]{2,1,0:T(2,128)} %pick_ref.1, s32[2,8]{1,0:T(2,128)} %bitcast.16, bf16[4,64,256]{2,1,0:T(8,128)(2,1)} %bitcast.10, bf16[4,64,256]{2,1,0:T(8,128)(2,1)} %bitcast.11, ...), custom_call_target="tpu_custom_call" | custom-call | tf_op jit(solution)/shard_map/pallas_call | solution.py:430
  45.3 1.8 %shard_map.104 = (bf16[4,64,256]{2,1,0:T(8,128)(2,1)}, bf16[4,64,256]{2,1,0:T(8,128)(2,1)}, bf16[4,64,256]{2,1,0:T(8,128)(2,1)}) custom-call(bf16[4,64,256]{2,1,0:T(8,128)(2,1)} %get-tuple-element.9.a_ref, bf16[4,64,256]{2,1,0:T(8,128)(2,1)} %get-tuple-element.10.b_ref, bf16[4,64,256]{2,1,0:T(8,128)(2,1)} %get-tuple-element.11.c_ref), custom_call_target="tpu_custom_call" | custom-call | tf_op jit(solution)/shard_map/pallas_call | solution.py:476

commit v4 on v3

--- a/solution.py
+++ b/solution.py
@@ -47,7 +47,7 @@
     for t in range(1, heads):
         pl.semaphore_signal(barrier, inc=1, device_id={"head": (me_h + t) % heads, "seq": me_s})
 
-    @pl.loop(1, seqs)
+    @pl.loop(1, half + 1)
     def _(i):
         pl.semaphore_signal(barrier, inc=1, device_id={"head": me_h, "seq": mate(i)})
 
@@ -94,7 +94,7 @@
         line = jnp.concatenate([lse_ref[:, x * rows:(x + 1) * rows] * LOG2E] * CAP, axis=1)
         lz[x] = jnp.where(row == 0, jnp.broadcast_to(line, (metas, wide)), 0.0)
 
-    pl.semaphore_wait(barrier, heads - 1 + seqs - 1)
+    pl.semaphore_wait(barrier, heads - 1 + half)
 
     def head_copy(t, n):
         to = (me_h + t) % heads
@@ -121,6 +121,7 @@
 
     owners.start()
     far_part(0, 0).start()
+    far_part(1, 0).start()
     for n in (0, 1, 4, 2, 3):
         for t in range(1, heads):
             head_copy(t, n).start()
@@ -151,7 +152,6 @@
     for t in range(1, heads):
         head_copy(t, 0).wait_recv()
         far_part(0, t).start()
-    far_part(1, 0).start()
     for t in range(1, heads):
         head_copy(t, 1).wait_recv()
         far_part(1, t).start()

time: 47.3 us -> 49.4 us (1.044)
  Pallas kernels: 46.4 us -> 48.6 us
    pallas_call x1, Pallas kernels: 44.6 us -> 46.8 us  [on_device(): pl.pallas_call(functools.partial(kernel, heads, seqs, sel), out_shape=[ja...]
where the time goes in v4:
time: 49.4 us; the launch traced here: 49.2 us
  Pallas kernels  48.6 us (98%)
  between operations  0.64 us (1%)
    pallas_call x1, Pallas kernels, on_device(): pl.pallas_call(functools.partial(kernel, heads, seqs, sel), out_shape=[ja...  46.8 us
    pallas_call x1, Pallas kernels, on_device(): pl.pallas_call(place, out_shape=[jax.ShapeDtypeStruct((piece, rows, full)...  1.8 us

profile of v4, /device:TPU:0, one launch (start us, length us, event | category | flops | bytes accessed | tf_op | source)
XLA Modules:
  0.0 49.2 jit_solution(4410417428391473770)
XLA Ops:
  0.6 46.8 %shard_map.103 = (bf16[4,64,256]{2,1,0:T(8,128)(2,1)}, bf16[4,64,256]{2,1,0:T(8,128)(2,1)}, bf16[4,64,256]{2,1,0:T(8,128)(2,1)}) custom-call(s32[2,8]{1,0:T(2,128)} %bitcast.15, s32[8,2,8]{2,1,0:T(2,128)} %pick_ref.1, s32[2,8]{1,0:T(2,128)} %bitcast.16, bf16[4,64,256]{2,1,0:T(8,128)(2,1)} %bitcast.10, bf16[4,64,256]{2,1,0:T(8,128)(2,1)} %bitcast.11, ...), custom_call_target="tpu_custom_call" | custom-call | tf_op jit(solution)/shard_map/pallas_call | solution.py:430
  47.4 1.8 %shard_map.104 = (bf16[4,64,256]{2,1,0:T(8,128)(2,1)}, bf16[4,64,256]{2,1,0:T(8,128)(2,1)}, bf16[4,64,256]{2,1,0:T(8,128)(2,1)}) custom-call(bf16[4,64,256]{2,1,0:T(8,128)(2,1)} %get-tuple-element.9.a_ref, bf16[4,64,256]{2,1,0:T(8,128)(2,1)} %get-tuple-element.10.b_ref, bf16[4,64,256]{2,1,0:T(8,128)(2,1)} %get-tuple-element.11.c_ref), custom_call_target="tpu_custom_call" | custom-call | tf_op jit(solution)/shard_map/pallas_call | solution.py:476
